TPU v7x, 32 devices: a whole 2x2x4 slice. The times are simulated.
32 devices in a mesh: sp: 16 (over z, y, x), pb: 2 (over core).
Axes of the slice: x: 2, y: 2, z: 4, core: 2. Of those that a mesh axis runs over, the one named last changes fastest.
Arguments:
- amplitudes: bfloat16 [40, 1024, 1024], P('pb', 'sp'), may hold values from -6 to 6
- virtuals: bfloat16 [1400, 1024], replicated, may hold values from -0.375 to 0.375
- energies: float32 [1024], replicated, may hold values from 0.02 to 0.2
- integrals: bfloat16 [2048, 2048], P('sp'), may hold values from -0.125 to 0.125
- screened: int32 [16, 16], P('sp'), may hold values from 0 to 15, as said below
- counts: int32 [16], P('sp'), may hold values from 1 to 16, 128 in all
- offsets: int32 [2, 16], replicated, may hold values from 0 to 1384
- coupling: bfloat16 [40, 40], P('pb'), may hold values from -1 to 1
Outputs:
- residual: bfloat16 [40, 1024, 1024], P('pb', 'sp')
Inputs may be any that keep to these rules, and one draw needn't show every extreme that they name: `screened`: each row names 16 different blocks.
All inputs are finite; a program needn't handle non-finite values. No bound on the sum of `counts` on one device may be relied on, other than what follows from the above.
Results may differ from a plain program's by a relative error of at most 0.01.
Values may be sent and summed in bfloat16 or wider, within the bound.
No kernel may reach another device: no remote copies, remote signals or barrier semaphores. Data moves between devices by JAX's collectives and lax.ppermute only.
A program may use at most 64 MiB of HBM per device.

v0:
```python
import jax
import jax.numpy as jnp
from jax import lax
from jax.sharding import PartitionSpec as P

SHELL_ROW = 8
SHELL_COL = 16


def shards(amplitudes, virtuals, energies, integrals, screened, counts, offsets, coupling):
    pairs = amplitudes.shape[0]
    ext_rows = amplitudes.shape[1]
    width = SHELL_ROW * SHELL_COL
    nblk = lax.axis_size("sp")
    first = lax.axis_index("sp") * ext_rows
    local_cols = lax.dynamic_slice_in_dim(virtuals, first, ext_rows, 1)
    half = jnp.einsum(
        "pab,nb->pan", amplitudes, virtuals, preferred_element_type=jnp.float32
    ).astype(jnp.bfloat16)
    row_span = jnp.arange(SHELL_ROW, dtype=jnp.int32)
    col_span = jnp.arange(SHELL_COL, dtype=jnp.int32)
    lows = offsets[0]
    highs = offsets[1]
    left = local_cols[lows[:, None] + row_span[None, :]]
    right = half[:, :, highs[:, None] + col_span[None, :]]
    term = jnp.einsum("bia,pabs->bpis", left, right, preferred_element_type=jnp.float32)
    ao_all = lax.psum(term.reshape(nblk, pairs, width), "sp").astype(jnp.bfloat16)
    slots = screened.shape[1]
    live = (jnp.arange(slots, dtype=jnp.int32) < counts[0]).astype(jnp.bfloat16)
    chosen = jnp.take(ao_all, screened[0], axis=0) * live[:, None, None]
    slab = integrals.reshape(width, slots, width)
    raw = jnp.einsum("rkc,kpc->pr", slab, chosen, preferred_element_type=jnp.float32).astype(
        jnp.bfloat16
    )
    every = lax.all_gather(raw[None], ("sp", "pb"), axis=0, tiled=True)
    every = every.reshape(nblk, coupling.shape[1], width)
    k_all = jnp.einsum("pq,bqc->bpc", coupling, every, preferred_element_type=jnp.float32).astype(
        jnp.bfloat16
    )
    left_all = local_cols[offsets[0][:, None] + row_span[None, :]]
    right_rows = virtuals[offsets[1][:, None] + col_span[None, :]]
    square = k_all.reshape(nblk, pairs, SHELL_ROW, SHELL_COL)
    upper = jnp.einsum(
        "bia,bpis->pabs", left_all, square, preferred_element_type=jnp.float32
    ).astype(jnp.bfloat16)
    inner = jnp.einsum("pabs,bsn->pan", upper, right_rows, preferred_element_type=jnp.float32)
    own_energy = lax.dynamic_slice_in_dim(energies, first, ext_rows)
    diag = own_energy[:, None] + energies[None, :]
    return (inner + diag[None] * amplitudes.astype(jnp.float32)).astype(jnp.bfloat16)


def solution(mesh):
    return jax.shard_map(
        shards,
        mesh=mesh,
        in_specs=(
            P("pb", "sp", None),
            P(),
            P(),
            P("sp", None),
            P("sp", None),
            P("sp"),
            P(),
            P("pb", None),
        ),
        out_specs=P("pb", "sp", None),
        check_vma=False,
    )
```

profile of v0, /device:TPU:0, one launch (start us, length us, event | category | flops | bytes accessed | tf_op | source)
XLA Modules:
  0.0 168.3 jit_solution(11485403471382570395)
XLA Ops:
  0.0 0.0 copy-start
  0.0 1.8 %copy-done = bf16[1400,1024]{1,0:T(8,128)(2,1)S(1)} copy-done((bf16[1400,1024]{1,0:T(8,128)(2,1)S(1)}, bf16[1400,1024]{1,0:T(8,128)(2,1)}, u32[]{:S(2)}) %copy-start) | copy-done | bytes 2867224
  1.8 0.2 constant_dynamic-slice_fusion
  2.0 0.8 slice_bitcast_fusion
  2.7 0.1 compare_select_fusion
  2.8 0.1 reshape.178
  2.9 0.7 gather_fusion.1
  3.6 0.1 compare_select_fusion.1
  3.7 0.1 reshape.170
  3.8 0.0 copy-start.1
  3.8 7.6 %convolution_convert_fusion = bf16[20,64,1400]{2,1,0:T(8,128)(2,1)} fusion(bf16[20,64,1024]{2,1,0:T(8,128)(2,1)} %param.8, bf16[1400,1024]{1,0:T(8,128)(2,1)S(1)} %copy-done), kind=kOutput, calls=%fused_computation.6 | convolution fusion | flops 3671808000 | bytes 9072640 | tf_op jit(solution)/shard_map/pab,nb->pan/dot_general | solution.py:17
  11.4 10.8 %copy.25 = bf16[20,64,1400]{1,0,2:T(8,128)(2,1)} copy(bf16[20,64,1400]{2,1,0:T(8,128)(2,1)} %convolution_convert_fusion) | data formatting | bytes 7168000 | tf_op jit(solution)/shard_map/convert_element_type | solution.py:19
  22.1 0.0 copy-done.1
  22.2 5.5 %gather_fusion = bf16[256,20,64]{2,1,0:T(8,128)(2,1)} fusion(bf16[20,64,1400]{1,0,2:T(8,128)(2,1)} %copy.25, s32[1024]{0:T(1024)S(1)} %pad_clamp_fusion.2), kind=kCustom, calls=%fused_computation | custom fusion | bytes 1311744 | tf_op jit(solution)/shard_map/gather | solution.py:25
  27.6 0.0 copy-start.3
  27.6 5.1 %convolution_bitcast_fusion = f32[16,20,8,16]{1,2,3,0:T(8,128)} fusion(bf16[20,64,16,16]{1,0,3,2:T(8,128)(2,1)} %bitcast.75, bf16[128,64]{1,0:T(8,128)(2,1)S(1)} %gather_fusion.1), kind=kOutput, calls=%fused_computation.10 | convolution fusion | flops 5242880 | bytes 835584 | tf_op jit(solution)/shard_map/bia,pabs->bpis/dot_general | solution.py:26
  32.7 0.0 copy-start.2
  32.7 3.2 %copy.35 = f32[16,20,8,16]{3,2,1,0:T(8,128)} copy(f32[16,20,8,16]{1,2,3,0:T(8,128)} %convolution_bitcast_fusion) | data formatting | bytes 327680 | tf_op jit(solution)/shard_map/reshape | solution.py:27
  35.9 1.7 %reshape.214 = f32[16,20,128]{2,1,0:T(8,128)S(1)} reshape(f32[16,20,8,16]{3,2,1,0:T(8,128)} %copy.35) | data formatting | bytes 327680 | tf_op jit(solution)/shard_map/reshape | solution.py:27
  37.6 80.3 %all-reduce.1 = bf16[16,20,128]{2,1,0:T(8,128)(2,1)S(1)} all-reduce(f32[16,20,128]{2,1,0:T(8,128)S(1)} %reshape.214), channel_id=1, replica_groups=mesh['sp'=16,'pb'=2] {'sp'}, use_global_device_ids=true, to_apply=%region_0.0 | all-reduce | flops 40960 | bytes 245760 | tf_op jit(solution)/shard_map/psum | solution.py:27
  117.9 0.0 copy-done.3
  117.9 0.6 gather_fusion.2
  119.2 1.3 fusion.5
  120.5 36.9 %all-gather.1 = bf16[32,20,128]{2,1,0:T(8,128)(2,1)S(1)} all-gather(bf16[1,20,128]{2,1,0:T(8,128)(2,1)S(1)} %fusion.5), channel_id=2, replica_groups=mesh['sp'=16,'pb'=2] {'sp','pb'}, dimensions={0}, use_global_device_ids=true | all-gather | bytes 168960 | tf_op jit(solution)/shard_map/all_gather | solution.py:35
  157.4 0.0 copy-done.2
  157.4 0.2 fusion.3
  157.6 0.6 copy.31
  158.2 1.3 reshape.167
  159.6 0.8 dynamic_slice.7
  160.3 1.5 broadcast_add_fusion
  161.8 2.1 %gather_fusion.3 = bf16[256,1024]{1,0:T(8,128)(2,1)} fusion(bf16[1400,1024]{1,0:T(8,128)(2,1)S(1)} %copy-done, s32[1024]{0:T(1024)} %copy-done.1), kind=kCustom, calls=%fused_computation.3 | custom fusion | bytes 1049600 | tf_op jit(solution)/shard_map/gather | solution.py:41
  163.9 4.4 %fusion = bf16[20,64,1024]{2,1,0:T(8,128)(2,1)} fusion(bf16[20,64,1024]{2,1,0:T(8,128)(2,1)} %param.8, f32[64,1024]{1,0:T(8,128)} %broadcast_add_fusion, bf16[16,16,1024,1]{2,1,0,3:T(8,128)(2,1)} %bitcast.76, bf16[16,20,8,16]{3,2,0,1:T(8,128)(2,1)S(1)} %reshape.167, bf16[128,64]{1,0:T(8,128)(2,1)S(1)} %gather_fusion.1), kind=kOutput, calls=%fused_computation.5 | convolution fusion | flops 681902080 | bytes 6127616 | tf_op jit(solution)/shard_map/pabs,bsn->pan/dot_general | solution.py:46
  (6 shorter events, 0.1 us)
Async XLA Ops:
  0.0 1.8 %copy-start = (bf16[1400,1024]{1,0:T(8,128)(2,1)S(1)}, bf16[1400,1024]{1,0:T(8,128)(2,1)}, u32[]{:S(2)}) copy-start(bf16[1400,1024]{1,0:T(8,128)(2,1)} %param.9) | copy-start | bytes 8601604
  3.8 18.4 %copy-start.1 = (s32[1024]{0:T(1024)}, s32[1024]{0:T(1024)S(1)}, u32[]{:S(2)}) copy-start(s32[1024]{0:T(1024)S(1)} %pad_clamp_fusion.2) | copy-start | bytes 12292
  27.6 90.3 %copy-start.3 = (s32[1,16]{1,0:T(1,128)S(1)}, s32[1,16]{1,0:T(1,128)}, u32[]{:S(2)}) copy-start(s32[1,16]{1,0:T(1,128)} %param.12) | copy-start | bytes 196
  32.7 124.7 %copy-start.2 = (bf16[20,40]{1,0:T(8,128)(2,1)S(1)}, bf16[20,40]{1,0:T(8,128)(2,1)}, u32[]{:S(2)}) copy-start(bf16[20,40]{1,0:T(8,128)(2,1)} %param.15) | copy-start | bytes 4804
where the time goes:
time: 169 us; the launch traced here: 168 us
  blocking collectives  117 us (69%)
  local copies, waits for them, and re-layouts  30.2 us (18%)
  matrix products  18.6 us (11%)
    psum x1, blocking collectives, shards(): lax.psum(term.reshape(nblk, pairs, width), 'sp').astype(jnp.bfloat16)  80.3 us
    all_gather x1, blocking collectives, shards(): every = lax.all_gather(raw[None], ('sp', 'pb'), axis=0, tiled=True)  36.9 us
    convert_element_type x1, local copies, waits for them, and re-layouts, shards(): half = jnp.einsum('pab,nb->pan', amplitudes, virtuals, preferred_element_...  10.8 us
    dot_general x1, matrix products, shards(): jnp.einsum('pab,nb->pan', amplitudes, virtuals, preferred_element_type=jn...  7.57 us
    gather x1, local copies, waits for them, and re-layouts, shards(): right = half[:, :, highs[:, None] + col_span[None, :]]  5.49 us
    dot_general x1, matrix products, shards(): jnp.einsum('bia,pabs->bpis', left, right, preferred_element_type=jnp.floa...  5.06 us
    reshape x2, local copies, waits for them, and re-layouts, shards(): term.reshape(nblk, pairs, width)  4.85 us
    dot_general x1, matrix products, shards(): jnp.einsum('pabs,bsn->pan', upper, right_rows, preferred_element_type=jnp...  4.45 us

commit v1 on v0

--- a/solution.py
+++ b/solution.py
@@ -5,6 +5,13 @@
 
 SHELL_ROW = 8
 SHELL_COL = 16
+
+
+def swapped_in(x, axis, along):
+    n_dev = lax.axis_size(axis)
+    blocks = jnp.stack([x for _ in range(n_dev)])
+    blocks = lax.all_to_all(blocks, axis, split_axis=0, concat_axis=0)
+    return jnp.concatenate(blocks, axis=along)
 
 
 def shards(amplitudes, virtuals, energies, integrals, screened, counts, offsets, coupling):
@@ -32,7 +39,7 @@
     raw = jnp.einsum("rkc,kpc->pr", slab, chosen, preferred_element_type=jnp.float32).astype(
         jnp.bfloat16
     )
-    every = lax.all_gather(raw[None], ("sp", "pb"), axis=0, tiled=True)
+    every = swapped_in(raw[None], ("sp", "pb"), 0)
     every = every.reshape(nblk, coupling.shape[1], width)
     k_all = jnp.einsum("pq,bqc->bpc", coupling, every, preferred_element_type=jnp.float32).astype(
         jnp.bfloat16

time: 169 us -> 139 us (0.82)
  blocking collectives: 117 us -> 80.3 us
  waiting for transfers between devices: 0 us -> 6.14 us
  starting transfers between devices: 0 us -> 2.71 us
    all_gather x1 -> x0, blocking collectives: 36.9 us -> none  [shards(): every = lax.all_gather(raw[None], ('sp', 'pb'), axis=0, tiled=True)]
    all_to_all x0 -> x1, waiting for transfers between devices: none -> 6.14 us  [swapped_in(): blocks = lax.all_to_all(blocks, axis, split_axis=0, concat_axis=0)]
    all_to_all x0 -> x1, starting transfers between devices: none -> 2.71 us  [swapped_in(): blocks = lax.all_to_all(blocks, axis, split_axis=0, concat_axis=0)]
  transfers between devices with their start and end apart: 0 -> 1, of which waited for: 0 -> 1; matrix products, arithmetic and copies ran while one was open for 0% -> 2% of each run, Pallas kernels for 0% -> 0%
where the time goes in v1:
time: 139 us; the launch traced here: 138 us
  blocking collectives  80.3 us (58%)
  local copies, waits for them, and re-layouts  29 us (21%)
  matrix products  18.5 us (13%)
  waiting for transfers between devices  6.14 us (4%)
  starting transfers between devices  2.71 us (2%)
    psum x1, blocking collectives, shards(): lax.psum(term.reshape(nblk, pairs, width), 'sp').astype(jnp.bfloat16)  80.3 us
    convert_element_type x1, local copies, waits for them, and re-layouts, shards(): half = jnp.einsum('pab,nb->pan', amplitudes, virtuals, preferred_element_...  10.7 us
    dot_general x1, matrix products, shards(): jnp.einsum('pab,nb->pan', amplitudes, virtuals, preferred_element_type=jn...  7.47 us
    all_to_all x1, waiting for transfers between devices, swapped_in(): blocks = lax.all_to_all(blocks, axis, split_axis=0, concat_axis=0)  6.14 us
    gather x1, local copies, waits for them, and re-layouts, shards(): right = half[:, :, highs[:, None] + col_span[None, :]]  5.49 us
    dot_general x1, matrix products, shards(): jnp.einsum('bia,pabs->bpis', left, right, preferred_element_type=jnp.floa...  5.07 us
    reshape x2, local copies, waits for them, and re-layouts, shards(): term.reshape(nblk, pairs, width)  4.84 us
    dot_general x1, matrix products, shards(): jnp.einsum('pabs,bsn->pan', upper, right_rows, preferred_element_type=jnp...  4.45 us
  transfers between devices with their start and end apart: 1, of which 1 were waited for; matrix products, arithmetic and copies ran while one was open for 2% of the time, Pallas kernels for 0%

profile of v1, /device:TPU:0, one launch (start us, length us, event | category | flops | bytes accessed | tf_op | source)
XLA Modules:
  0.0 138.3 jit_solution(8747100655846738503)
XLA Ops:
  0.0 0.0 copy-start
  0.0 0.8 slice_bitcast_fusion
  0.9 0.1 compare_select_fusion
  0.9 0.1 reshape.176
  1.0 0.1 compare_select_fusion.1
  1.1 0.1 reshape.168
  1.2 0.6 copy-done
  1.8 0.2 constant_dynamic-slice_fusion
  2.0 7.5 %convolution_convert_fusion = bf16[20,64,1400]{2,1,0:T(8,128)(2,1)} fusion(bf16[20,64,1024]{2,1,0:T(8,128)(2,1)} %param.8, bf16[1400,1024]{1,0:T(8,128)(2,1)S(1)} %copy-done), kind=kOutput, calls=%fused_computation.6 | convolution fusion | flops 3671808000 | bytes 9072640 | tf_op jit(solution)/shard_map/pab,nb->pan/dot_general | solution.py:24
  9.5 10.7 %copy.25 = bf16[20,64,1400]{1,0,2:T(8,128)(2,1)} copy(bf16[20,64,1400]{2,1,0:T(8,128)(2,1)} %convolution_convert_fusion) | data formatting | bytes 7168000 | tf_op jit(solution)/shard_map/convert_element_type | solution.py:26
  20.2 0.7 gather_fusion.1
  20.9 5.5 %gather_fusion = bf16[256,20,64]{2,1,0:T(8,128)(2,1)} fusion(bf16[20,64,1400]{1,0,2:T(8,128)(2,1)} %copy.25, s32[1024]{0:T(1024)S(1)} %pad_clamp_fusion.2), kind=kCustom, calls=%fused_computation | custom fusion | bytes 1311744 | tf_op jit(solution)/shard_map/gather | solution.py:32
  26.4 0.0 copy-start.3
  26.4 5.1 %convolution_bitcast_fusion = f32[16,20,8,16]{1,2,3,0:T(8,128)} fusion(bf16[20,64,16,16]{1,0,3,2:T(8,128)(2,1)} %bitcast.71, bf16[128,64]{1,0:T(8,128)(2,1)S(1)} %gather_fusion.1), kind=kOutput, calls=%fused_computation.10 | convolution fusion | flops 5242880 | bytes 835584 | tf_op jit(solution)/shard_map/bia,pabs->bpis/dot_general | solution.py:33
  31.5 3.2 %copy.35 = f32[16,20,8,16]{3,2,1,0:T(8,128)} copy(f32[16,20,8,16]{1,2,3,0:T(8,128)} %convolution_bitcast_fusion) | data formatting | bytes 327680 | tf_op jit(solution)/shard_map/reshape | solution.py:34
  34.7 1.7 %reshape.207 = f32[16,20,128]{2,1,0:T(8,128)S(1)} reshape(f32[16,20,8,16]{3,2,1,0:T(8,128)} %copy.35) | data formatting | bytes 327680 | tf_op jit(solution)/shard_map/reshape | solution.py:34
  36.3 80.3 %all-reduce.1 = bf16[16,20,128]{2,1,0:T(8,128)(2,1)S(1)} all-reduce(f32[16,20,128]{2,1,0:T(8,128)S(1)} %reshape.207), channel_id=1, replica_groups=mesh['sp'=16,'pb'=2] {'sp'}, use_global_device_ids=true, to_apply=%region_0.0 | all-reduce | flops 40960 | bytes 245760 | tf_op jit(solution)/shard_map/psum | solution.py:34
  116.7 0.0 copy-done.3
  117.4 0.6 gather_fusion.2
  118.0 0.0 copy-start.2
  118.0 1.3 fusion.4
  119.3 0.7 stack.3
  120.0 0.0 copy-start.1
  120.0 2.7 %all-to-all-start = ((bf16[32,1,20,128]{3,2,1,0:T(8,128)(2,1)}), bf16[32,1,20,128]{3,2,1,0:T(8,128)(2,1)S(1)}, u32[]{:S(2)}, u32[]{:S(2)}) async-start(bf16[32,1,20,128]{3,2,1,0:T(8,128)(2,1)} %stack.3), calls=%async_computation | async-start | bytes 393216 | tf_op jit(solution)/shard_map/all_to_all | solution.py:13
  122.8 2.0 %gather_fusion.3 = bf16[256,1024]{1,0:T(8,128)(2,1)} fusion(bf16[1400,1024]{1,0:T(8,128)(2,1)S(1)} %copy-done, s32[1024]{0:T(1024)S(1)} %pad_clamp_fusion.2), kind=kCustom, calls=%fused_computation.3 | custom fusion | bytes 1049600 | tf_op jit(solution)/shard_map/gather | solution.py:48
  124.7 0.0 copy-done.2
  124.7 0.1 dynamic_slice.7
  124.8 0.8 broadcast_add_fusion
  125.6 6.1 %all-to-all-done = bf16[32,1,20,128]{3,2,1,0:T(8,128)(2,1)S(1)} async-done(((bf16[32,1,20,128]{3,2,1,0:T(8,128)(2,1)}), bf16[32,1,20,128]{3,2,1,0:T(8,128)(2,1)S(1)}, u32[]{:S(2)}, u32[]{:S(2)}) %all-to-all-start) | async-done | bytes 163872 | tf_op jit(solution)/shard_map/all_to_all | solution.py:13
  131.7 0.0 copy-done.1
  131.8 0.2 fusion.3
  131.9 0.6 copy.31
  132.6 1.3 reshape.165
  133.9 4.4 %fusion = bf16[20,64,1024]{2,1,0:T(8,128)(2,1)} fusion(bf16[20,64,1024]{2,1,0:T(8,128)(2,1)} %param.8, f32[64,1024]{1,0:T(8,128)} %broadcast_add_fusion, bf16[16,16,1024,1]{2,1,0,3:T(8,128)(2,1)} %bitcast.72, bf16[16,20,8,16]{3,2,0,1:T(8,128)(2,1)S(1)} %reshape.165, bf16[128,64]{1,0:T(8,128)(2,1)S(1)} %gather_fusion.1), kind=kOutput, calls=%fused_computation.5 | convolution fusion | flops 681902080 | bytes 6127616 | tf_op jit(solution)/shard_map/pabs,bsn->pan/dot_general | solution.py:53
  (6 shorter events, 0.1 us)
Async XLA Ops:
  0.0 1.8 %copy-start = (bf16[1400,1024]{1,0:T(8,128)(2,1)S(1)}, bf16[1400,1024]{1,0:T(8,128)(2,1)}, u32[]{:S(2)}) copy-start(bf16[1400,1024]{1,0:T(8,128)(2,1)} %param.9) | copy-start | bytes 8601604
  26.4 90.3 %copy-start.3 = (s32[1,16]{1,0:T(1,128)S(1)}, s32[1,16]{1,0:T(1,128)}, u32[]{:S(2)}) copy-start(s32[1,16]{1,0:T(1,128)} %param.12) | copy-start | bytes 196
  118.0 6.7 %copy-start.2 = (f32[1024]{0:T(1024)S(1)}, f32[1024]{0:T(1024)}, u32[]{:S(2)}) copy-start(f32[1024]{0:T(1024)} %param.10) | copy-start | bytes 12292
  120.0 11.7 %copy-start.1 = (bf16[20,40]{1,0:T(8,128)(2,1)S(1)}, bf16[20,40]{1,0:T(8,128)(2,1)}, u32[]{:S(2)}) copy-start(bf16[20,40]{1,0:T(8,128)(2,1)} %param.15) | copy-start | bytes 4804
  120.0 11.7 %all-to-all-start = ((bf16[32,1,20,128]{3,2,1,0:T(8,128)(2,1)}), bf16[32,1,20,128]{3,2,1,0:T(8,128)(2,1)S(1)}, u32[]{:S(2)}, u32[]{:S(2)}) async-start(bf16[32,1,20,128]{3,2,1,0:T(8,128)(2,1)} %stack.3), calls=%async_computation | async-start | bytes 393216 | tf_op jit(solution)/shard_map/all_to_all | solution.py:13
